TPU v7x, 256 devices: a whole 4x4x8 slice. The times are simulated.
256 devices in a mesh: doc: 32 (over y, x, core), term: 4 (over z_lo), pair: 2 (over z_hi).
Axes of the slice: x: 4, y: 4, z: 8 (z_hi: 2, z_lo: 4; z = z_hi * 4 + z_lo), core: 2. Of those that a mesh axis runs over, the one named last changes fastest.
Arguments:
- counts: int32 [64, 16, 128, 128], P('doc', 'term'), may hold values from 0 to 11
- block_ids: int32 [64, 16], P('doc', 'term'), may hold values from 0 to 8191, as said below
- live_slots: int32 [64, 16], P('doc', 'term'), may hold values 0 or 1
- lengths: int32 [8192], P('doc'), may hold values from 1 to 24528, as said below
- pairs: int32 [4096, 2], P(('doc', 'pair')), may hold values from 0 to 63, as said below
- pair_count: int32 [64], P(('doc', 'pair')), may hold values from 1 to 64, as said below
Outputs:
- gram: float32 [4096, 128, 128], P(('doc', 'pair'), 'term')
Inputs may be any that keep to these rules, and one draw needn't show every extreme that they name: `block_ids`: columns s * 4 to (s + 1) * 4 - 1 hold term blocks of the s-th of 4 equal ranges of the 8192 blocks, distinct within one document block and range. `lengths`: document b * 128 + r has a length of the sum of counts[b, s, r, t] over all slots s and all t plus tokens outside its blocks: 1 to 2000 of them for every document but the last, whose length is exactly 24528. `pairs`: the left block of row k belongs to doc index k // 128. Rows k with k % 64 < pair_count[k // 64] are live; some entry equals 64.
All inputs are finite; a program needn't handle non-finite values. No bound on the sum of `live_slots` on one device may be relied on, other than what follows from the above.
Results may differ from a plain program's by a relative error of at most 0.0014.
Values may be sent and summed in bfloat16 or wider, within the bound.
No kernel may reach another device: no remote copies, remote signals or barrier semaphores. Data moves between devices by JAX's collectives and lax.ppermute only.
A program may use at most 64 MiB of HBM per device.

v0:
```python
import jax
import jax.numpy as jnp
from jax import lax
from jax.sharding import PartitionSpec as P

V = 1048576
PB = 8


saturation = 1.2
length_weight = 0.75
epsilon = 1e-06


def gram_block(normalized, block_ids, whole_tiles, whole_ids, pair_batch, left_base):
    left_index = pair_batch[:, 0] - left_base
    right_pair_index = pair_batch[:, 1]
    left_tiles = normalized[left_index]
    right_tiles = whole_tiles[right_pair_index]
    matches = (block_ids[left_index][:, :, None] == whole_ids[right_pair_index][:, None, :]).astype(
        jnp.bfloat16
    )
    aligned = jnp.einsum(
        "pij,pjet->piet", matches, right_tiles, preferred_element_type=jnp.float32
    ).astype(jnp.bfloat16)
    return jnp.einsum("pidt,piet->pde", left_tiles, aligned, preferred_element_type=jnp.float32)


def run_pairs(work_pairs, work_count, normalized, block_ids, whole_tiles, whole_ids, left_base):
    capacity = work_pairs.shape[0]
    doc_rows = normalized.shape[2]
    step_count = (work_count + PB - 1) // PB

    def pair_step(loop_index, partial_value):
        first_row = loop_index * PB
        pair_batch = lax.dynamic_slice_in_dim(work_pairs, first_row, PB, 0)
        gram_tiles = gram_block(
            normalized, block_ids, whole_tiles, whole_ids, pair_batch, left_base
        )
        live_mask = first_row + jnp.arange(PB, dtype=jnp.int32) < work_count
        gram_tiles = jnp.where(live_mask[:, None, None], gram_tiles, 0.0)
        return lax.dynamic_update_slice_in_dim(partial_value, gram_tiles, first_row, 0)

    return lax.fori_loop(
        0, step_count, pair_step, jnp.zeros((capacity, doc_rows, doc_rows), jnp.float32)
    )


def shards(counts, block_ids, live_slots, lengths, pairs, pair_count):
    block_count, slot_count, doc_rows, term_columns = counts.shape
    covered_blocks = V // term_columns // lax.axis_size("term")
    local_ids = block_ids - lax.axis_index("term") * covered_blocks
    present = (counts > 0) & (live_slots[:, :, None, None] > 0)
    col_docs = jnp.sum(present.astype(jnp.float32), axis=2)
    freq_part = (
        jnp.zeros((covered_blocks, term_columns), jnp.float32)
        .at[local_ids.reshape(-1)]
        .add(col_docs.reshape(-1, term_columns))
    )
    len_float = lengths.astype(jnp.float32)
    doc_freq, len_total = (
        lax.psum(freq_part.astype(jnp.bfloat16), "doc").astype(jnp.float32),
        lax.psum(jnp.sum(len_float).astype(jnp.bfloat16), "doc").astype(jnp.float32),
    )
    docs_all = len_float.shape[0] * lax.axis_size("doc")
    avg_len = len_total / docs_all
    inv_freq = jnp.log(1.0 + (docs_all - doc_freq + 0.5) / (doc_freq + 0.5))
    slot_freq = inv_freq[local_ids]
    len_scale = (
        1.0
        - length_weight
        + length_weight * len_float.reshape(block_count, 1, doc_rows, 1) / avg_len
    )
    term_freq = counts.astype(jnp.float32)
    weight = jnp.where(
        present,
        slot_freq[:, :, None, :]
        * term_freq
        * (saturation + 1.0)
        / (term_freq + saturation * len_scale),
        0.0,
    )
    square_sum = lax.psum(jnp.sum(weight * weight, axis=(1, 3)), "term")
    normalized = (weight * lax.rsqrt(square_sum + epsilon)[:, None, :, None]).astype(jnp.bfloat16)
    whole_tiles, whole_ids = (
        lax.all_gather(normalized, "doc", axis=0, tiled=True),
        lax.all_gather(block_ids, "doc", axis=0, tiled=True),
    )
    left_base = lax.axis_index("doc") * block_count
    own_count = pair_count[0]
    partial_value = run_pairs(
        pairs, own_count, normalized, block_ids, whole_tiles, whole_ids, left_base
    )
    own_grams = lax.psum_scatter(partial_value, "term", scatter_dimension=1, tiled=True)
    return own_grams


def solution(mesh):
    in_specs = (
        P("doc", "term", None, None),
        P("doc", "term"),
        P("doc", "term"),
        P("doc"),
        P(("doc", "pair"), None),
        P(("doc", "pair")),
    )
    out_specs = P(("doc", "pair"), "term", None)
    return jax.shard_map(shards, mesh=mesh, in_specs=in_specs, out_specs=out_specs, check_vma=False)
```

profile of v0, /device:TPU:32, one launch (start us, length us, event | category | flops | bytes accessed | tf_op | source)
XLA Modules:
  0.0 360.6 jit_solution(16410767193192183070)
XLA Ops:
  6.5 0.7 broadcast_compare_fusion
  7.3 0.7 compare_select_fusion.2
  8.0 0.1 reshape.67
  8.1 1.2 convert_reduce_fusion
  9.2 0.9 scatter_custom_fusion
  10.1 0.8 convert_element_type.29
  11.0 0.0 all-reduce.2.cloned.1.call-update
  11.0 0.0 all-gather.3.cloned.1.call-start
  11.1 1.4 convert_reduce_fusion.1
  12.4 0.1 reshape.103
  12.5 67.9 %psum.22 = bf16[]{:T(256)} all-reduce(bf16[]{:T(256)} %convert_reduce_fusion.1), channel_id=1, replica_groups=mesh['doc'=32,'term'=4,'pair'=2] {'doc'}, use_global_device_ids=true, to_apply=%region_4.0 | all-reduce | flops 1 | bytes 4 | tf_op jit(solution)/shard_map/psum | solution.py:63
  81.2 0.7 multiply_bitcast_fusion
  81.9 46.3 %all-reduce.2.cloned.1.call-done = bf16[2048,128]{1,0:T(8,128)(2,1)} async-done(((bf16[2048,128]{1,0:T(8,128)(2,1)}), bf16[2048,128]{1,0:T(8,128)(2,1)}) %all-reduce.2.cloned.1.call-update) | async-done | bytes 524304 | tf_op jit(solution)/shard_map/psum | solution.py:62
  128.2 1.3 fusion.12
  129.5 0.6 gather_fusion.4
  130.1 0.4 multiply_reduce_fusion
  130.5 9.0 %psum.23 = f32[2,128]{1,0:T(2,128)S(1)} all-reduce(f32[2,128]{1,0:T(2,128)S(1)} %multiply_reduce_fusion), channel_id=1, replica_groups=mesh['doc'=32,'term'=4,'pair'=2] {'term'}, use_global_device_ids=true, to_apply=%region_6.7 | all-reduce | flops 256 | bytes 2048 | tf_op jit(solution)/shard_map/psum | solution.py:83
  139.5 1.0 multiply_convert_fusion
  140.5 0.0 reduce-scatter.2.cloned.1.call-start
  141.3 24.7 %all-gather = s32[32,2,4]{2,1,0:T(2,128)S(1)} all-gather(s32[1,2,4]{2,1,0:T(2,128)S(1)} %bitcast.35), channel_id=1, replica_groups=mesh['doc'=32,'term'=4,'pair'=2] {'doc'}, dimensions={0}, use_global_device_ids=true | all-gather | bytes 1056 | tf_op jit(solution)/shard_map/all_gather | solution.py:87
  165.9 32.1 %all-gather.3.cloned.1.call-done = bf16[64,4,128,128]{3,2,1,0:T(8,128)(2,1)} async-done(((bf16[2,4,128,128]{3,2,1,0:T(8,128)(2,1)}), bf16[64,4,128,128]{3,2,1,0:T(8,128)(2,1)}) %all-gather.3.cloned.1.call-update) | async-done | bytes 8388624 | tf_op jit(solution)/shard_map/all_gather | solution.py:86
  198.1 2.5 broadcast_in_dim.18
  200.6 9.1 %while.10 = (s32[]{:T(128)}, f32[64,128,128]{2,1,0:T(8,128)}, s32[]{:T(128)}, s32[]{:T(128)}, s32[64,2]{0,1:T(2,128)S(1)}, /*index=5*/s32[]{:T(128)}, bf16[2,4,1...) while((s32[]{:T(128)}, f32[64,128,128]{2,1,0:T(8,128)}, ...), condition=%wide.region_8.9_spmd, body=%wide.region_7.8_spmd.sunk | while | flops 138545360 | bytes 8922519 | solution.py:44
  200.6 0.7 add_compare_fusion.2
  201.2 0.1 constant_dynamic-slice_fusion.2
  201.3 0.6 gather_fusion.3
  201.9 0.6 gather_fusion.2
  202.5 4.1 %gather_fusion.1 = bf16[8,4,128,128]{3,2,1,0:T(8,128)(2,1)S(1)} fusion(bf16[64,4,128,128]{3,2,1,0:T(8,128)(2,1)} %get-tuple-element.192, s32[1024]{0:T(1024)S(1)} %get-tuple-element.154), kind=kCustom, calls=%fused_computation.3.clone.1 | custom fusion | bytes 2097184 | tf_op jit(solution)/shard_map/while/body/gather | solution.py:19
  206.6 1.0 fusion.27
  207.6 0.7 gather_fusion
  208.3 1.3 fusion.28
  209.7 144.4 %reduce-scatter.2.cloned.1.call-done = f32[64,32,128]{2,1,0:T(8,128)} async-done(((f32[64,128,128]{2,1,0:T(8,128)}), f32[64,32,128]{2,1,0:T(8,128)}) %reduce-scatter.2.cloned.1.call-update) | async-done | bytes 1048592 | tf_op jit(solution)/shard_map/reduce_scatter | solution.py:94
  (16 shorter events, 0.1 us)
Async XLA Ops:
  6.5 134.7 %copy-start.1 = (s32[2,4]{1,0:T(2,128)S(1)}, s32[2,4]{1,0:T(2,128)}, u32[]{:S(2)}) copy-start(s32[2,4]{1,0:T(2,128)} %param.9) | copy-start | bytes 100
  6.5 123.6 %copy-start.2 = (s32[2,4,128,128]{3,2,1,0:T(8,128)S(1)}, s32[2,4,128,128]{3,2,1,0:T(8,128)}, u32[]{:S(2)}) copy-start(s32[2,4,128,128]{3,2,1,0:T(8,128)} %param.8) | copy-start | bytes 1572868
  6.5 121.7 %all-reduce.2.cloned.1.call-start = ((), (), s32[]{:S(2)}) async-start(), calls=%async_computation.1 | async-start | bytes 1048576 | tf_op jit(solution)/shard_map/psum | solution.py:62
  11.0 189.6 %copy-start.3 = (s32[64,2]{0,1:T(2,128)S(1)}, s32[64,2]{0,1:T(2,128)}, u32[]{:S(2)}) copy-start(s32[64,2]{0,1:T(2,128)} %param.12) | copy-start | bytes 1540
  11.0 187.1 %all-gather.3.cloned.1.call-start = ((), (), s32[]{:S(2)}) async-start(), calls=%async_computation.2 | async-start | bytes 8650752 | tf_op jit(solution)/shard_map/all_gather | solution.py:86
  140.5 60.1 %copy-start = (bf16[2,4,128,128]{3,2,1,0:T(8,128)(2,1)S(1)}, bf16[2,4,128,128]{3,2,1,0:T(8,128)(2,1)}, u32[]{:S(2)}) copy-start(bf16[2,4,128,128]{3,2,1,0:T(8,128)(2,1)} %multiply_convert_fusion) | copy-start | bytes 786436
  140.5 213.6 %reduce-scatter.2.cloned.1.call-start = ((), (), s32[]{:S(2)}) async-start(), calls=%async_computation.3 | async-start | bytes 5242880 | tf_op jit(solution)/shard_map/reduce_scatter | solution.py:94
Sparse Core Ops, SparseCore 0:
  11.1 117.0 all-reduce.1
  140.6 57.3 all-gather.2
  209.8 144.2 reduce-scatter.1
where the time goes:
time: 362 us; the launch traced here: 361 us
  waiting for transfers between devices  223 us (62%)
  blocking collectives  102 us (28%)
  between operations  14.5 us (4%)
  other arithmetic  9.83 us (3%)
  local copies, waits for them, and re-layouts  9.29 us (3%)
    reduce_scatter x1, waiting for transfers between devices, shards(): lax.psum_scatter(partial_value, 'term', scatter_dimension=1, tiled=True)  144 us
    psum x1, blocking collectives, shards(): lax.psum(jnp.sum(len_float).astype(jnp.bfloat16), 'doc').astype(jnp.float32)  67.9 us
    psum x1, waiting for transfers between devices, shards(): lax.psum(freq_part.astype(jnp.bfloat16), 'doc').astype(jnp.float32)  46.3 us
    all_gather x1, waiting for transfers between devices, shards(): lax.all_gather(normalized, 'doc', axis=0, tiled=True)  32.1 us
    all_gather x1, blocking collectives, shards(): lax.all_gather(block_ids, 'doc', axis=0, tiled=True)  24.7 us
    psum x1, blocking collectives, shards(): square_sum = lax.psum(jnp.sum(weight * weight, axis=(1, 3)), 'term')  8.97 us
  transfers between devices with their start and end apart: 3, of which 3 were waited for; matrix products, arithmetic and copies ran while one was open for 1% of the time, Pallas kernels for 0%

commit v1 on v0

v1 whole, which is shorter than its diff:
```python
import jax
import jax.numpy as jnp
from jax import lax
from jax.experimental import pallas as pl
from jax.experimental.pallas import tpu as pltpu
from jax.sharding import PartitionSpec as P

PAIRS_PER_STEP = 4
CHUNK = 16
GRAM_SCALE = 32768.0

saturation = 1.2
length_weight = 0.75
epsilon = 1e-06


def gram_kernel(left_sel, right_sel, own_ids, all_ids, live, left_ref, length_ref, norm_ref, *refs):
    tile_refs = refs[:PAIRS_PER_STEP]
    out_ref = refs[PAIRS_PER_STEP]
    slots = tile_refs[0].shape[1]
    step = pl.program_id(0)
    for p in range(PAIRS_PER_STEP):
        k = step * PAIRS_PER_STEP + p
        left = left_sel[k]
        right = right_sel[k]
        len_row = length_ref[pl.ds(right, 1), :]
        parts = []
        for i in range(slots):
            wanted = own_ids[left * slots + i]
            found = jnp.int32(0)
            place = jnp.int32(0)
            for j in range(slots):
                same = all_ids[right * slots + j] == wanted
                found = jnp.where(same, 1, found)
                place = jnp.where(same, j, place)
            c = tile_refs[p][0, place].astype(jnp.float32)
            f = c / (c + len_row)
            parts.append((f * found.astype(jnp.float32)).astype(jnp.bfloat16))
        right_tile = jnp.concatenate(parts, axis=0)
        gram = jnp.dot(left_ref[left], right_tile, preferred_element_type=jnp.float32)
        scale = norm_ref[pl.ds(right, 1), :] * (live[k].astype(jnp.float32) * GRAM_SCALE)
        out_ref[p] = gram * scale


def gram_chunk(left_sel, right_sel, own_ids, all_ids, live, left_tiles, len_rows, norm_rows, tiles):
    pairs = left_sel.shape[0]
    blocks, slots, terms, rows = tiles.shape
    tile_specs = [
        pl.BlockSpec(
            (1, slots, terms, rows),
            lambda s, ls, rs, oi, ai, lv, p=p: (rs[s * PAIRS_PER_STEP + p], 0, 0, 0),
        )
        for p in range(PAIRS_PER_STEP)
    ]
    whole = lambda a: pl.BlockSpec(a.shape, lambda s, *_: (0,) * a.ndim)
    return pl.pallas_call(
        gram_kernel,
        grid_spec=pltpu.PrefetchScalarGridSpec(
            num_scalar_prefetch=5,
            grid=(pairs // PAIRS_PER_STEP,),
            in_specs=[whole(left_tiles), whole(len_rows), whole(norm_rows)] + tile_specs,
            out_specs=pl.BlockSpec((PAIRS_PER_STEP, rows, rows), lambda s, *_: (s, 0, 0)),
        ),
        out_shape=jax.ShapeDtypeStruct((pairs, rows, rows), jnp.float32),
        name="gram",
    )(
        left_sel, right_sel, own_ids, all_ids, live, left_tiles, len_rows, norm_rows,
        *([tiles] * PAIRS_PER_STEP),
    )


def shards(counts, block_ids, live_slots, lengths, pairs, pair_count):
    blocks, slots, rows, terms = counts.shape
    n_doc = lax.axis_size("doc")
    n_term = lax.axis_size("term")
    term_at = lax.axis_index("term")
    docs_all = lengths.shape[0] * n_doc
    own_slots = blocks * slots

    live_counts = jnp.where(live_slots[:, :, None, None] > 0, counts, 0)
    send_tiles = jnp.swapaxes(live_counts, 2, 3).astype(jnp.bfloat16)
    all_tiles = lax.all_gather(send_tiles, "doc", axis=0, tiled=True)

    col_docs = jnp.sum((live_counts > 0).astype(jnp.int32), axis=2).reshape(own_slots, terms)
    own_ids = block_ids.reshape(-1)
    small = jnp.concatenate(
        [
            col_docs,
            lengths.reshape(blocks, rows),
            jnp.pad(own_ids, (0, terms - own_slots)).reshape(1, terms),
        ],
        axis=0,
    )
    small_all = lax.all_gather(small, "doc", axis=0)
    col_all = small_all[:, :own_slots].reshape(n_doc * own_slots, terms)
    len_all = small_all[:, own_slots : own_slots + blocks].reshape(n_doc * blocks, rows)
    all_ids = small_all[:, own_slots + blocks, :own_slots].reshape(-1)

    same_ids = (own_ids[:, None] == all_ids[None, :]).astype(jnp.bfloat16)
    doc_freq = jnp.dot(same_ids, col_all.astype(jnp.bfloat16), preferred_element_type=jnp.float32)
    inv_freq = jnp.log(1.0 + (docs_all - doc_freq + 0.5) / (doc_freq + 0.5))
    idf = (inv_freq * (saturation + 1.0)).reshape(blocks, slots, 1, terms)
    avg_len = jnp.sum(len_all).astype(jnp.float32) / docs_all
    len_rows = saturation * (
        1.0 - length_weight + length_weight * len_all.astype(jnp.float32) / avg_len
    )
    own_len = saturation * (
        1.0 - length_weight + length_weight * lengths.astype(jnp.float32) / avg_len
    )
    own_c = live_counts.astype(jnp.float32)
    weight = idf * own_c / (own_c + own_len.reshape(blocks, 1, rows, 1))
    square_sum = lax.psum(jnp.sum(weight * weight, axis=(1, 3)), "term")
    norm = lax.rsqrt(square_sum + epsilon)
    left_tiles = (weight * idf * norm[:, None, :, None]).astype(jnp.bfloat16)
    left_tiles = jnp.swapaxes(left_tiles, 1, 2).reshape(blocks, rows, slots * terms)
    norm_rows = lax.all_gather(norm, "doc", axis=0, tiled=True)

    left_sel = pairs[:, 0] - lax.axis_index("doc") * blocks
    right_sel = pairs[:, 1]
    pair_slots = pairs.shape[0]
    live = (jnp.arange(pair_slots, dtype=jnp.int32) < pair_count[0]).astype(jnp.int32)
    rows_each = rows // n_term
    results = []
    for first in range(0, pair_slots, CHUNK):
        span = slice(first, first + CHUNK)
        grams = gram_chunk(
            left_sel[span], right_sel[span], own_ids, all_ids, live[span],
            left_tiles, len_rows, norm_rows, all_tiles,
        )
        cut = lambda to: lax.dynamic_slice_in_dim(grams, to * rows_each, rows_each, 1)
        total = cut(term_at)
        for shift in range(1, n_term):
            message = cut((term_at + shift) % n_term).astype(jnp.float16)
            got = lax.ppermute(
                message, "term", [(a, (a + shift) % n_term) for a in range(n_term)]
            )
            total = total + got.astype(jnp.float32)
        results.append(total * (1.0 / GRAM_SCALE))
    return jnp.concatenate(results, axis=0)


def solution(mesh):
    in_specs = (
        P("doc", "term", None, None),
        P("doc", "term"),
        P("doc", "term"),
        P("doc"),
        P(("doc", "pair"), None),
        P(("doc", "pair")),
    )
    out_specs = P(("doc", "pair"), "term", None)
    return jax.shard_map(shards, mesh=mesh, in_specs=in_specs, out_specs=out_specs, check_vma=False)
```

time: 362 us -> 152 us (0.42)
  waiting for transfers between devices: 223 us -> 15.3 us
  blocking collectives: 102 us -> 60 us
  Pallas kernels: 0 us -> 21.3 us
  starting transfers between devices: 0.09 us -> 19 us
  other arithmetic: 9.83 us -> 15.3 us
  local copies, waits for them, and re-layouts: 9.29 us -> 5.15 us
    reduce_scatter x1 -> x0, waiting for transfers between devices: 144 us -> none  [shards(): lax.psum_scatter(partial_value, 'term', scatter_dimension=1, tiled=True)]
    psum x1 -> x0, blocking collectives: 67.9 us -> none  [shards(): lax.psum(jnp.sum(len_float).astype(jnp.bfloat16), 'doc').astype(jnp.float32)]
    psum x1 -> x0, waiting for transfers between devices: 46.3 us -> none  [shards(): lax.psum(freq_part.astype(jnp.bfloat16), 'doc').astype(jnp.float32)]
    all_gather x1, waiting for transfers between devices: 32.1 us -> 0.01 us  [shards(): all_tiles = lax.all_gather(send_tiles, 'doc', axis=0, tiled=True)]
    all_gather x1 -> x2, blocking collectives: 24.7 us -> 50.7 us  [the longest x1 25.5 us: shards(): norm_rows = lax.all_gather(norm, 'doc', axis=0, tiled=True)]
    pallas_call x0 -> x4, Pallas kernels: none -> 21.3 us  [gram_chunk(): pl.pallas_call(gram_kernel, grid_spec=pltpu.PrefetchScalarGridSpec(num_sc...]
    ppermute x0 -> x12, starting transfers between devices: none -> 19 us  [shards(): lax.ppermute(message, 'term', [(a, (a + shift) % n_term) for a in range(n...]
    ppermute x0 -> x12, waiting for transfers between devices: none -> 15.3 us  [shards(): lax.ppermute(message, 'term', [(a, (a + shift) % n_term) for a in range(n...]
  transfers between devices with their start and end apart: 3 -> 13, of which waited for: 3 -> 5; matrix products, arithmetic and copies ran while one was open for 1% -> 10% of each run, Pallas kernels for 0% -> 11%
where the time goes in v1:
time: 152 us; the launch traced here: 151 us
  blocking collectives  60 us (39%)
  Pallas kernels  21.3 us (14%)
  starting transfers between devices  19 us (12%)
  other arithmetic  15.3 us (10%)
  waiting for transfers between devices  15.3 us (10%)
  between operations  14.9 us (10%)
  local copies, waits for them, and re-layouts  5.15 us (3%)
    all_gather x1, blocking collectives, shards(): norm_rows = lax.all_gather(norm, 'doc', axis=0, tiled=True)  25.5 us
    all_gather x1, blocking collectives, shards(): small_all = lax.all_gather(small, 'doc', axis=0)  25.1 us
    pallas_call x4, Pallas kernels, gram_chunk(): pl.pallas_call(gram_kernel, grid_spec=pltpu.PrefetchScalarGridSpec(num_sc...  21.3 us
    ppermute x12, starting transfers between devices, shards(): lax.ppermute(message, 'term', [(a, (a + shift) % n_term) for a in range(n...  19 us
    ppermute x12, waiting for transfers between devices, shards(): lax.ppermute(message, 'term', [(a, (a + shift) % n_term) for a in range(n...  15.3 us
    psum x1, blocking collectives, shards(): square_sum = lax.psum(jnp.sum(weight * weight, axis=(1, 3)), 'term')  9.34 us
    convert_element_type x4, other arithmetic, shards(): message = cut((term_at + shift) % n_term).astype(jnp.float16)  4.73 us
    mul x4, other arithmetic, shards(): results.append(total * (1.0 / GRAM_SCALE))  4.1 us
  transfers between devices with their start and end apart: 13, of which 5 were waited for; matrix products, arithmetic and copies ran while one was open for 10% of the time, Pallas kernels for 11%

profile of v1, /device:TPU:32, one launch (start us, length us, event | category | flops | bytes accessed | tf_op | source)
XLA Modules:
  0.0 151.1 jit_solution(290844724685218949)
XLA Ops:
  6.5 1.2 copy.23
  8.5 0.9 fusion
  10.9 25.1 %all-gather.1 = s32[32,11,128]{2,1,0:T(8,128)S(1)} all-gather(s32[1,11,128]{2,1,0:T(8,128)S(1)} %add_bitcast_fusion), channel_id=2, replica_groups=mesh['doc'=32,'term'=4,'pair'=2] {'doc'}, dimensions={0}, use_global_device_ids=true | all-gather | bytes 185856 | tf_op jit(solution)/shard_map/all_gather | solution.py:94
  38.6 9.3 %psum.7 = f32[2,128]{1,0:T(2,128)S(1)} all-reduce(f32[2,128]{1,0:T(2,128)S(1)} %multiply_reduce_fusion), channel_id=1, replica_groups=mesh['doc'=32,'term'=4,'pair'=2] {'term'}, use_global_device_ids=true, to_apply=%region_3.4 | all-reduce | flops 256 | bytes 2048 | tf_op jit(solution)/shard_map/psum | solution.py:112
  48.2 0.9 copy.25.left_ref
  49.7 25.5 %all-gather.2 = f32[32,2,128]{2,1,0:T(2,128)} all-gather(f32[1,2,128]{2,1,0:T(2,128)S(1)} %get-tuple-element.23), channel_id=1, replica_groups=mesh['doc'=32,'term'=4,'pair'=2] {'doc'}, dimensions={0}, use_global_device_ids=true | all-gather | bytes 33792 | tf_op jit(solution)/shard_map/all_gather | solution.py:116
  76.6 1.5 slice_bitcast_fusion.6
  78.7 5.4 %gram.4 = f32[16,128,128]{2,1,0:T(8,128)} custom-call(s32[16]{0:T(128)} %get-tuple-element.36.left_sel, s32[16]{0:T(128)} %get-tuple-element.19.right_sel, s32[8]{0:T(128)} %copy-done.1, s32[256]{0:T(256)} %copy-done, s32[16]{0:T(128)} %get-tuple-element.25.live, bf16[2,128,512]{2,1,0:T(8,128)(2,1)} %copy.25.left_ref, f32[64,128]{1,0:T(8,128)} %bitcast.46, ...), custom_call_target="tpu_custom_call" | custom-call | tf_op jit(solution)/shard_map/gram/pallas_call | solution.py:56
  84.1 1.2 dynamic-slice_convert_fusion.11
  85.3 2.0 %collective-permute-start = (f16[16,32,128]{2,1,0:T(8,128)(2,1)S(1)}, f16[16,32,128]{2,1,0:T(8,128)(2,1)S(1)}, u32[]{:S(2)}, u32[]{:S(2)}) collective-permute-start(f16[16,32,128]{2,1,0:T(8,128)(2,1)S(1)} %get-tuple-element.5), channel_id=1, source_target_pairs={{0,2},{2,4},{4,6},{6,0},{1,3},{3,5},{5,7},{7,1},{8,10},{10,12},{12... | collective-permute-start | bytes 393224 | tf_op jit(solution)/shard_map/ppermute | solution.py:134
  87.3 4.2 %collective-permute-start.1 = (f16[16,32,128]{2,1,0:T(8,128)(2,1)S(1)}, f16[16,32,128]{2,1,0:T(8,128)(2,1)S(1)}, u32[]{:S(2)}, u32[]{:S(2)}) collective-permute-start(f16[16,32,128]{2,1,0:T(8,128)(2,1)S(1)} %get-tuple-element.7), channel_id=1, source_target_pairs={{0,4},{2,6},{4,0},{6,2},{1,5},{3,7},{5,1},{7,3},{8,12},{10,14},{12... | collective-permute-start | bytes 393224 | tf_op jit(solution)/shard_map/ppermute | solution.py:134
  91.5 5.3 %gram.5 = f32[16,128,128]{2,1,0:T(8,128)} custom-call(s32[16]{0:T(128)} %get-tuple-element.33.left_sel, s32[16]{0:T(128)} %get-tuple-element.20.right_sel, s32[8]{0:T(128)} %copy-done.1, s32[256]{0:T(256)} %copy-done, s32[16]{0:T(128)} %get-tuple-element.28.live, bf16[2,128,512]{2,1,0:T(8,128)(2,1)} %copy.25.left_ref, f32[64,128]{1,0:T(8,128)} %bitcast.47, ...), custom_call_target="tpu_custom_call" | custom-call | tf_op jit(solution)/shard_map/gram/pallas_call | solution.py:56
  96.8 1.2 dynamic-slice_convert_fusion.8
  98.0 2.1 %collective-permute-start.3 = (f16[16,32,128]{2,1,0:T(8,128)(2,1)S(1)}, f16[16,32,128]{2,1,0:T(8,128)(2,1)S(1)}, u32[]{:S(2)}, u32[]{:S(2)}) collective-permute-start(f16[16,32,128]{2,1,0:T(8,128)(2,1)S(1)} %get-tuple-element.8), channel_id=1, source_target_pairs={{0,2},{2,4},{4,6},{6,0},{1,3},{3,5},{5,7},{7,1},{8,10},{10,12},{12... | collective-permute-start | bytes 393224 | tf_op jit(solution)/shard_map/ppermute | solution.py:134
  100.1 1.8 %collective-permute-start.4 = (f16[16,32,128]{2,1,0:T(8,128)(2,1)S(1)}, f16[16,32,128]{2,1,0:T(8,128)(2,1)S(1)}, u32[]{:S(2)}, u32[]{:S(2)}) collective-permute-start(f16[16,32,128]{2,1,0:T(8,128)(2,1)S(1)} %get-tuple-element.10), channel_id=1, source_target_pairs={{0,4},{2,6},{4,0},{6,2},{1,5},{3,7},{5,1},{7,3},{8,12},{10,14},{12... | collective-permute-start | bytes 393224 | tf_op jit(solution)/shard_map/ppermute | solution.py:134
  101.9 5.3 %gram.6 = f32[16,128,128]{2,1,0:T(8,128)} custom-call(s32[16]{0:T(128)} %get-tuple-element.34.left_sel, s32[16]{0:T(128)} %get-tuple-element.22.right_sel, s32[8]{0:T(128)} %copy-done.1, s32[256]{0:T(256)} %copy-done, s32[16]{0:T(128)} %get-tuple-element.27.live, bf16[2,128,512]{2,1,0:T(8,128)(2,1)} %copy.25.left_ref, f32[64,128]{1,0:T(8,128)} %bitcast.48, ...), custom_call_target="tpu_custom_call" | custom-call | tf_op jit(solution)/shard_map/gram/pallas_call | solution.py:56
  107.2 1.2 dynamic-slice_convert_fusion.5
  108.4 5.3 %gram.7 = f32[16,128,128]{2,1,0:T(8,128)} custom-call(s32[16]{0:T(128)} %get-tuple-element.35.left_sel, s32[16]{0:T(128)} %get-tuple-element.21.right_sel, s32[8]{0:T(128)} %copy-done.1, s32[256]{0:T(256)} %copy-done, s32[16]{0:T(128)} %get-tuple-element.26.live, bf16[2,128,512]{2,1,0:T(8,128)(2,1)} %copy.25.left_ref, f32[64,128]{1,0:T(8,128)} %bitcast.49, ...), custom_call_target="tpu_custom_call" | custom-call | tf_op jit(solution)/shard_map/gram/pallas_call | solution.py:56
  113.7 1.2 dynamic-slice_convert_fusion.2
  115.0 2.0 %collective-permute-start.6 = (f16[16,32,128]{2,1,0:T(8,128)(2,1)S(1)}, f16[16,32,128]{2,1,0:T(8,128)(2,1)S(1)}, u32[]{:S(2)}, u32[]{:S(2)}) collective-permute-start(f16[16,32,128]{2,1,0:T(8,128)(2,1)S(1)} %get-tuple-element.11), channel_id=1, source_target_pairs={{0,2},{2,4},{4,6},{6,0},{1,3},{3,5},{5,7},{7,1},{8,10},{10,12},{12... | collective-permute-start | bytes 393224 | tf_op jit(solution)/shard_map/ppermute | solution.py:134
  117.0 2.9 %collective-permute-start.7 = (f16[16,32,128]{2,1,0:T(8,128)(2,1)S(1)}, f16[16,32,128]{2,1,0:T(8,128)(2,1)S(1)}, u32[]{:S(2)}, u32[]{:S(2)}) collective-permute-start(f16[16,32,128]{2,1,0:T(8,128)(2,1)S(1)} %get-tuple-element.13), channel_id=1, source_target_pairs={{0,4},{2,6},{4,0},{6,2},{1,5},{3,7},{5,1},{7,3},{8,12},{10,14},{12... | collective-permute-start | bytes 393224 | tf_op jit(solution)/shard_map/ppermute | solution.py:134
  119.9 1.0 add_multiply_fusion.3
  121.9 6.5 %collective-permute-done.5 = f16[16,32,128]{2,1,0:T(8,128)(2,1)S(1)} collective-permute-done((f16[16,32,128]{2,1,0:T(8,128)(2,1)S(1)}, f16[16,32,128]{2,1,0:T(8,128)(2,1)S(1)}, u32[]{:S(2)}, u32[]{:S(2)}) %collective-permute-start.5) | collective-permute-done | bytes 131104 | tf_op jit(solution)/shard_map/ppermute | solution.py:134
  128.3 1.0 add_multiply_fusion.2
  129.4 2.2 %collective-permute-done.6 = f16[16,32,128]{2,1,0:T(8,128)(2,1)S(1)} collective-permute-done((f16[16,32,128]{2,1,0:T(8,128)(2,1)S(1)}, f16[16,32,128]{2,1,0:T(8,128)(2,1)S(1)}, u32[]{:S(2)}, u32[]{:S(2)}) %collective-permute-start.6) | collective-permute-done | bytes 131104 | tf_op jit(solution)/shard_map/ppermute | solution.py:134
  131.6 3.0 %collective-permute-start.9 = (f16[16,32,128]{2,1,0:T(8,128)(2,1)S(1)}, f16[16,32,128]{2,1,0:T(8,128)(2,1)S(1)}, u32[]{:S(2)}, u32[]{:S(2)}) collective-permute-start(f16[16,32,128]{2,1,0:T(8,128)(2,1)S(1)} %get-tuple-element.14), channel_id=1, source_target_pairs={{0,2},{2,4},{4,6},{6,0},{1,3},{3,5},{5,7},{7,1},{8,10},{10,12},{12... | collective-permute-start | bytes 393224 | tf_op jit(solution)/shard_map/ppermute | solution.py:134
  134.5 1.8 %collective-permute-done.7 = f16[16,32,128]{2,1,0:T(8,128)(2,1)S(1)} collective-permute-done((f16[16,32,128]{2,1,0:T(8,128)(2,1)S(1)}, f16[16,32,128]{2,1,0:T(8,128)(2,1)S(1)}, u32[]{:S(2)}, u32[]{:S(2)}) %collective-permute-start.7) | collective-permute-done | bytes 131104 | tf_op jit(solution)/shard_map/ppermute | solution.py:134
  136.4 1.8 %collective-permute-done.8 = f16[16,32,128]{2,1,0:T(8,128)(2,1)S(1)} collective-permute-done((f16[16,32,128]{2,1,0:T(8,128)(2,1)S(1)}, f16[16,32,128]{2,1,0:T(8,128)(2,1)S(1)}, u32[]{:S(2)}, u32[]{:S(2)}) %collective-permute-start.8) | collective-permute-done | bytes 131104 | tf_op jit(solution)/shard_map/ppermute | solution.py:134
  138.2 1.0 add_multiply_fusion.1
  139.2 3.0 %collective-permute-done.11 = f16[16,32,128]{2,1,0:T(8,128)(2,1)S(1)} collective-permute-done((f16[16,32,128]{2,1,0:T(8,128)(2,1)S(1)}, f16[16,32,128]{2,1,0:T(8,128)(2,1)S(1)}, u32[]{:S(2)}, u32[]{:S(2)}) %collective-permute-start.11) | collective-permute-done | bytes 131104 | tf_op jit(solution)/shard_map/ppermute | solution.py:134
  142.2 1.0 add_multiply_fusion
  143.2 1.0 pad_maximum_fusion
  (35 shorter events, 7.3 us)
Async XLA Ops:
  6.5 72.2 %all-gather.5.cloned.1.call-start = ((), (), s32[]{:S(2)}) async-start(), calls=%async_computation | async-start | bytes 8650752 | tf_op jit(solution)/shard_map/all_gather | solution.py:82
  10.2 68.6 %copy-start.1 = (s32[8]{0:T(128)}, s32[8]{0:T(128)S(1)}, u32[]{:S(2)}) copy-start(s32[8]{0:T(128)S(1)} %reshape.44.own_ids) | copy-start | bytes 100
  36.1 42.6 %copy-start = (s32[256]{0:T(256)}, s32[256]{0:T(256)S(1)}, u32[]{:S(2)}) copy-start(s32[256]{0:T(256)S(1)} %reshape_squeeze.3.all_ids) | copy-start | bytes 3076
  85.3 29.6 %collective-permute-start = (f16[16,32,128]{2,1,0:T(8,128)(2,1)S(1)}, f16[16,32,128]{2,1,0:T(8,128)(2,1)S(1)}, u32[]{:S(2)}, u32[]{:S(2)}) collective-permute-start(f16[16,32,128]{2,1,0:T(8,128)(2,1)S(1)} %get-tuple-element.5), channel_id=1, source_target_pairs={{0,2},{2,4},{4,6},{6,0},{1,3},{3,5},{5,7},{7,1},{8,10},{10,12},{12... | collective-permute-start | bytes 393224 | tf_op jit(solution)/shard_map/ppermute | solution.py:134
  87.3 27.7 %collective-permute-start.1 = (f16[16,32,128]{2,1,0:T(8,128)(2,1)S(1)}, f16[16,32,128]{2,1,0:T(8,128)(2,1)S(1)}, u32[]{:S(2)}, u32[]{:S(2)}) collective-permute-start(f16[16,32,128]{2,1,0:T(8,128)(2,1)S(1)} %get-tuple-element.7), channel_id=1, source_target_pairs={{0,4},{2,6},{4,0},{6,2},{1,5},{3,7},{5,1},{7,3},{8,12},{10,14},{12... | collective-permute-start | bytes 393224 | tf_op jit(solution)/shard_map/ppermute | solution.py:134
  91.5 25.5 %collective-permute-start.2 = (f16[16,32,128]{2,1,0:T(8,128)(2,1)S(1)}, f16[16,32,128]{2,1,0:T(8,128)(2,1)S(1)}, u32[]{:S(2)}, u32[]{:S(2)}) collective-permute-start(f16[16,32,128]{2,1,0:T(8,128)(2,1)S(1)} %get-tuple-element.6), channel_id=1, source_target_pairs={{0,6},{2,0},{4,2},{6,4},{1,7},{3,1},{5,3},{7,5},{8,14},{10,8},{12,... | collective-permute-start | bytes 393224 | tf_op jit(solution)/shard_map/ppermute | solution.py:134
  98.0 22.9 %collective-permute-start.3 = (f16[16,32,128]{2,1,0:T(8,128)(2,1)S(1)}, f16[16,32,128]{2,1,0:T(8,128)(2,1)S(1)}, u32[]{:S(2)}, u32[]{:S(2)}) collective-permute-start(f16[16,32,128]{2,1,0:T(8,128)(2,1)S(1)} %get-tuple-element.8), channel_id=1, source_target_pairs={{0,2},{2,4},{4,6},{6,0},{1,3},{3,5},{5,7},{7,1},{8,10},{10,12},{12... | collective-permute-start | bytes 393224 | tf_op jit(solution)/shard_map/ppermute | solution.py:134
  100.1 21.1 %collective-permute-start.4 = (f16[16,32,128]{2,1,0:T(8,128)(2,1)S(1)}, f16[16,32,128]{2,1,0:T(8,128)(2,1)S(1)}, u32[]{:S(2)}, u32[]{:S(2)}) collective-permute-start(f16[16,32,128]{2,1,0:T(8,128)(2,1)S(1)} %get-tuple-element.10), channel_id=1, source_target_pairs={{0,4},{2,6},{4,0},{6,2},{1,5},{3,7},{5,1},{7,3},{8,12},{10,14},{12... | collective-permute-start | bytes 393224 | tf_op jit(solution)/shard_map/ppermute | solution.py:134
  114.9 13.5 %collective-permute-start.5 = (f16[16,32,128]{2,1,0:T(8,128)(2,1)S(1)}, f16[16,32,128]{2,1,0:T(8,128)(2,1)S(1)}, u32[]{:S(2)}, u32[]{:S(2)}) collective-permute-start(f16[16,32,128]{2,1,0:T(8,128)(2,1)S(1)} %get-tuple-element.9), channel_id=1, source_target_pairs={{0,6},{2,0},{4,2},{6,4},{1,7},{3,1},{5,3},{7,5},{8,14},{10,8},{12,... | collective-permute-start | bytes 393224 | tf_op jit(solution)/shard_map/ppermute | solution.py:134
  115.0 16.6 %collective-permute-start.6 = (f16[16,32,128]{2,1,0:T(8,128)(2,1)S(1)}, f16[16,32,128]{2,1,0:T(8,128)(2,1)S(1)}, u32[]{:S(2)}, u32[]{:S(2)}) collective-permute-start(f16[16,32,128]{2,1,0:T(8,128)(2,1)S(1)} %get-tuple-element.11), channel_id=1, source_target_pairs={{0,2},{2,4},{4,6},{6,0},{1,3},{3,5},{5,7},{7,1},{8,10},{10,12},{12... | collective-permute-start | bytes 393224 | tf_op jit(solution)/shard_map/ppermute | solution.py:134
  117.0 19.4 %collective-permute-start.7 = (f16[16,32,128]{2,1,0:T(8,128)(2,1)S(1)}, f16[16,32,128]{2,1,0:T(8,128)(2,1)S(1)}, u32[]{:S(2)}, u32[]{:S(2)}) collective-permute-start(f16[16,32,128]{2,1,0:T(8,128)(2,1)S(1)} %get-tuple-element.13), channel_id=1, source_target_pairs={{0,4},{2,6},{4,0},{6,2},{1,5},{3,7},{5,1},{7,3},{8,12},{10,14},{12... | collective-permute-start | bytes 393224 | tf_op jit(solution)/shard_map/ppermute | solution.py:134
  120.9 17.2 %collective-permute-start.8 = (f16[16,32,128]{2,1,0:T(8,128)(2,1)S(1)}, f16[16,32,128]{2,1,0:T(8,128)(2,1)S(1)}, u32[]{:S(2)}, u32[]{:S(2)}) collective-permute-start(f16[16,32,128]{2,1,0:T(8,128)(2,1)S(1)} %get-tuple-element.12), channel_id=1, source_target_pairs={{0,6},{2,0},{4,2},{6,4},{1,7},{3,1},{5,3},{7,5},{8,14},{10,8},{12,... | collective-permute-start | bytes 393224 | tf_op jit(solution)/shard_map/ppermute | solution.py:134
  121.2 18.0 %collective-permute-start.10 = (f16[16,32,128]{2,1,0:T(8,128)(2,1)S(1)}, f16[16,32,128]{2,1,0:T(8,128)(2,1)S(1)}, u32[]{:S(2)}, u32[]{:S(2)}) collective-permute-start(f16[16,32,128]{2,1,0:T(8,128)(2,1)S(1)} %get-tuple-element.16), channel_id=1, source_target_pairs={{0,4},{2,6},{4,0},{6,2},{1,5},{3,7},{5,1},{7,3},{8,12},{10,14},{12... | collective-permute-start | bytes 393224 | tf_op jit(solution)/shard_map/ppermute | solution.py:134
  128.3 13.9 %collective-permute-start.11 = (f16[16,32,128]{2,1,0:T(8,128)(2,1)S(1)}, f16[16,32,128]{2,1,0:T(8,128)(2,1)S(1)}, u32[]{:S(2)}, u32[]{:S(2)}) collective-permute-start(f16[16,32,128]{2,1,0:T(8,128)(2,1)S(1)} %get-tuple-element.15), channel_id=1, source_target_pairs={{0,6},{2,0},{4,2},{6,4},{1,7},{3,1},{5,3},{7,5},{8,14},{10,8},{12,... | collective-permute-start | bytes 393224 | tf_op jit(solution)/shard_map/ppermute | solution.py:134
  131.6 10.7 %collective-permute-start.9 = (f16[16,32,128]{2,1,0:T(8,128)(2,1)S(1)}, f16[16,32,128]{2,1,0:T(8,128)(2,1)S(1)}, u32[]{:S(2)}, u32[]{:S(2)}) collective-permute-start(f16[16,32,128]{2,1,0:T(8,128)(2,1)S(1)} %get-tuple-element.14), channel_id=1, source_target_pairs={{0,2},{2,4},{4,6},{6,0},{1,3},{3,5},{5,7},{7,1},{8,10},{10,12},{12... | collective-permute-start | bytes 393224 | tf_op jit(solution)/shard_map/ppermute | solution.py:134
Sparse Core Ops, SparseCore 0:
  9.9 60.6 all-gather.4
